TPU v7x, 32 devices: a whole 2x2x4 slice. The times are simulated.
32 devices in a mesh: sector: 16 (over z, y, x), dof: 2 (over core).
Axes of the slice: x: 2, y: 2, z: 4, core: 2. Of those that a mesh axis runs over, the one named last changes fastest.
Arguments:
- loads: bfloat16 [16, 128, 32768], P('sector', None, 'dof'), may hold values from -0.75 to 0.75
- modes: bfloat16 [32768, 512], P('dof'), may hold values from -0.25 to 0.25
- response: float32 [16, 128, 512], P('sector', None, 'dof'), may hold values from -6 to 6
- pattern: int32 [16], P('sector'), may hold values from 0 to 7
- deviation: float32 [8, 512], replicated, may hold values from -1 to 1
- eigen: float32 [16, 512], replicated, may hold values from 1 to 10
- loss: float32 [512], replicated, may hold values from 0.2 to 0.6
- omega_sq: float32 [64], replicated, may hold values from 0.5 to 12
- iface_left: int32 [1024], P('dof'), may hold values from 0 to 16383, as said below
- iface_right: int32 [1024], P('dof'), may hold values from 0 to 16383, as said below
Outputs:
- modal_response: float32 [16, 128, 512], P('sector', None, 'dof')
- displacement: bfloat16 [16, 128, 32768], P('sector', None, 'dof')
Inputs may be any that keep to these rules, and one draw needn't show every extreme that they name: Within each block of 512 entries, the entries of iface_left and of iface_right together are (2) * 512 distinct rows. `iface_right`: see iface_left.
All inputs are finite; a program needn't handle non-finite values.
Results may differ from a plain program's by a relative error of at most 0.005.
Values may be sent and summed in bfloat16 or wider, within the bound.
A program may use at most 128 MiB of HBM per device.

v0:
```python
import math

import jax
import jax.numpy as jnp
from jax import lax
from jax.sharding import PartitionSpec as P


def shifted_2(shard, axis, by):
    size = lax.axis_size(axis)
    return lax.ppermute(shard, axis, [(i, (i + by) % size) for i in range(size)])


def tables(row_count, col_count, sectors):
    rows_idx = jnp.arange(row_count, dtype=jnp.int32) % sectors
    cols_idx = jnp.arange(col_count, dtype=jnp.int32) % sectors
    turns = rows_idx[:, None] * cols_idx[None, :] % sectors
    theta = turns.astype(jnp.float32) * (2.0 * math.pi / sectors)
    return (jnp.cos(theta), jnp.sin(theta))


def divide(spec_re, spec_im, shifted, damped):
    denom = shifted * shifted + damped * damped
    return (
        (spec_re * shifted + spec_im * damped) / denom,
        (spec_im * shifted - spec_re * damped) / denom,
    )


def shards(
    loads, modes, response, pattern, deviation, eigen, loss, omega_sq, iface_left, iface_right
):
    highest = lax.Precision.HIGHEST
    local_sec, rows_two, dof_rows = loads.shape
    freqs = rows_two // 2
    modes_all = modes.shape[1]
    sec_devices = lax.axis_size("sector")
    sectors = sec_devices * local_sec
    half = modes_all // lax.axis_size("dof")
    width = freqs * half
    first_mode = lax.axis_index("dof") * half
    partial_force = jnp.dot(
        loads.reshape(local_sec * rows_two, dof_rows), modes, preferred_element_type=jnp.float32
    )
    force = lax.psum_scatter(
        partial_force.reshape(local_sec, rows_two, modes_all),
        "dof",
        scatter_dimension=2,
        tiled=True,
    )
    table_count = deviation.shape[0]
    dev_half = lax.dynamic_slice_in_dim(deviation, first_mode, half, 1)
    onehot = (pattern[:, None] == jnp.arange(table_count, dtype=jnp.int32)[None, :]).astype(
        jnp.float32
    )
    dev_rows = jnp.dot(onehot, dev_half, precision=highest)
    rest = (force - dev_rows[:, None, :] * response).reshape(local_sec, 2, width)
    columns = lax.all_to_all(rest, "sector", split_axis=2, concat_axis=0, tiled=True)
    share = width // sec_devices
    col_idx = lax.axis_index("sector") * share + jnp.arange(share, dtype=jnp.int32)
    freq_idx = col_idx // half
    mode_idx = first_mode + col_idx % half
    stiff = jnp.take(eigen, mode_idx, axis=1)
    shifted = stiff - jnp.take(omega_sq, freq_idx)[None, :]
    damped = jnp.take(loss, mode_idx)[None, :] * stiff
    cosine, sine = tables(sectors, sectors, sectors)
    spec_re = jnp.dot(cosine, columns[:, 0], precision=highest) + jnp.dot(
        sine, columns[:, 1], precision=highest
    )
    spec_im = jnp.dot(cosine, columns[:, 1], precision=highest) - jnp.dot(
        sine, columns[:, 0], precision=highest
    )
    solved_re, solved_im = divide(spec_re, spec_im, shifted, damped)
    out_re = (
        jnp.dot(cosine, solved_re, precision=highest) - jnp.dot(sine, solved_im, precision=highest)
    ) / sectors
    out_im = (
        jnp.dot(cosine, solved_im, precision=highest) + jnp.dot(sine, solved_re, precision=highest)
    ) / sectors
    updated = lax.all_to_all(
        jnp.stack([out_re, out_im], 1).astype(jnp.bfloat16),
        "sector",
        split_axis=0,
        concat_axis=2,
        tiled=True,
    ).astype(jnp.float32)
    modal_response = updated.reshape(local_sec, rows_two, half)
    rounded = modal_response.astype(jnp.bfloat16)
    raw = jnp.einsum(
        "skm,dm->skd",
        lax.all_gather(rounded, "dof", axis=2, tiled=True),
        modes,
        preferred_element_type=jnp.float32,
    ).astype(jnp.bfloat16)
    left_vals = jnp.take(raw, iface_left, axis=2)
    right_vals = jnp.take(raw, iface_right, axis=2)
    next_left = shifted_2(left_vals, "sector", -1)
    prev_right = shifted_2(right_vals, "sector", 1)
    left_after = jnp.concatenate([left_vals[1:], next_left], 0)
    right_before = jnp.concatenate([prev_right, right_vals[:-1]], 0)
    right_new = (0.5 * (right_vals.astype(jnp.float32) + left_after.astype(jnp.float32))).astype(
        jnp.bfloat16
    )
    left_new = (0.5 * (right_before.astype(jnp.float32) + left_vals.astype(jnp.float32))).astype(
        jnp.bfloat16
    )
    displacement = raw.at[:, :, iface_right].set(right_new).at[:, :, iface_left].set(left_new)
    return (modal_response, displacement)


def solution(mesh):
    placed = (
        P("sector", None, "dof"),
        P("dof", None),
        P("sector", None, "dof"),
        P("sector"),
        P(),
        P(),
        P(),
        P(),
        P("dof"),
        P("dof"),
    )
    return jax.shard_map(
        shards,
        mesh=mesh,
        in_specs=placed,
        out_specs=(P("sector", None, "dof"), P("sector", None, "dof")),
        check_vma=False,
    )
```

profile of v0, /device:TPU:0, one launch (start us, length us, event | category | flops | bytes accessed | tf_op | source)
XLA Modules:
  0.0 273.0 jit_solution(13463132247253687220)
XLA Ops:
  7.3 10.1 %fusion.2 = f32[1,128,512]{2,1,0:T(8,128)} fusion(bf16[16384,512]{1,0:T(8,128)(2,1)} %param.13, bf16[1,128,16384]{2,1,0:T(8,128)(2,1)} %param.12), kind=kOutput, calls=%fused_computation.9 | convolution fusion | flops 2147483648 | bytes 21233664 | tf_op jit(solution)/shard_map/dot_general | solution.py:42
  19.0 0.7 fusion.90
  19.8 0.7 fusion.91
  20.4 0.7 fusion.88
  21.2 0.7 fusion.89
  22.7 6.9 %gather_fusion.1 = f32[1024]{0:T(1024)S(1)} fusion(f32[512]{0:T(512)S(1)} %copy-done.1, s32[1024]{0:T(1024)S(1)} %broadcast_clamp_fusion), kind=kCustom, calls=%fused_computation.3 | custom fusion | bytes 12288 | tf_op jit(solution)/shard_map/jit(_take)/gather | solution.py:65
  29.7 4.4 %compare_select_fusion.2 = f32[1024,1]{0,1:T(1,128)S(1)} fusion(f32[]{:T(128)} %bitcast.69, f32[]{:T(128)} %bitcast.70, f32[]{:T(128)} %bitcast.71, f32[]{:T(128)} %bitcast.72, f32[]{:T(128)} %bitcast.73, f32[]{:T(128)} %bitcast.75, f32[]{:T(128)} %bitcast.74, s32[]{:T(128)S(6)} %mul.129), kind=kLoop, calls=%fused_computation.107 | loop fusion | flops 31744 | bytes 4128 | tf_op jit(solution)/shard_map/jit(_take)/gather | solution.py:64
  34.1 0.9 multiply_subtract_fusion
  35.1 12.0 %copy.32 = f32[1,2,16384]{1,0,2:T(1,128)} copy(f32[1,2,16384]{2,1,0:T(2,128)S(1)} %reshape.256) | data formatting | bytes 262144 | tf_op jit(solution)/shard_map/reshape | solution.py:57
  47.2 0.5 broadcast.1041
  47.7 74.5 %reduce.114 = f32[16384,2]{1,0:T(8,128)} reduce(f32[16384,1,2]{2,1,0:T(1,128)} %bitcast.171, f32[]{:T(128)} %broadcast.1041), dimensions={1}, to_apply=%bitcast.154.reduce_sub_computation | reduce | bytes 262148
  122.1 8.2 %reshape.603 = f32[16,1,2048]{2,1,0:T(1,128)} reshape(f32[16384,2]{1,0:T(8,128)} %reduce.114) | data formatting | bytes 262144
  130.4 8.4 %all-to-all-start = ((f32[16,1,2048]{2,1,0:T(1,128)}), f32[16,1,2048]{2,1,0:T(1,128)S(1)}, u32[]{:S(2)}, u32[]{:S(2)}) async-start(f32[16,1,2048]{2,1,0:T(1,128)} %reshape.603), calls=%async_computation.1 | async-start | bytes 262144 | tf_op jit(solution)/shard_map/all_to_all | solution.py:58
  138.9 2.8 %gather_fusion = f32[1024,16]{1,0:T(8,128)S(1)} fusion(f32[16,512]{0,1:T(8,128)S(1)} %copy.34, s32[1024]{0:T(1024)S(1)} %broadcast_clamp_fusion), kind=kCustom, calls=%fused_computation.2 | custom fusion | bytes 135168 | tf_op jit(solution)/shard_map/jit(_take)/gather | solution.py:63
  142.0 35.5 %select_select_fusion = f32[1024]{0:T(1024)S(1)} fusion(pred[1024]{0:T(1024)(128)(4,1)S(1)} %get-tuple-element.77, pred[1024]{0:T(1024)(128)(4,1)S(1)} %get-tuple-element.78, pred[1024]{0:T(1024)(128)(4,1)S(1)} %get-tuple-element.79, pred[1024]{0:T(1024)(128)(4,1)S(1)} %get-tuple-element.80, pred[1024]{0:T(1024)(128)(4,1)S(1)} %get-tuple-element.81, ...), kind=kLoop, calls=%fused_computation.141 | loop fusion | flops 81920 | bytes 66792 | tf_op jit(solution)/shard_map/jit(_take)/select_n | solution.py:64
  177.6 1.0 reduce.115
  178.5 14.7 %reshape.604 = f32[16384,1,2]{2,1,0:T(1,128)} reshape(f32[16,2048]{1,0:T(8,128)S(1)} %reduce.115) | data formatting | bytes 262144
  193.3 5.2 %copy.42 = f32[1,2,16,1024]{3,2,1,0:T(8,128)S(1)} copy(f32[1,2,16,1024]{1,3,2,0:T(8,128)} %bitcast.172) | data formatting | bytes 262144 | tf_op jit(solution)/shard_map/all_to_all | solution.py:58
  201.1 0.7 copy.36
  201.8 6.9 %all-to-all-start.1 = ((bf16[16,2,1024]{2,1,0:T(2,128)(2,1)}), bf16[16,2,1024]{2,1,0:T(2,128)(2,1)S(1)}, u32[]{:S(2)}, u32[]{:S(2)}) async-start(bf16[16,2,1024]{2,1,0:T(2,128)(2,1)} %copy.36), calls=%async_computation.2 | async-start | bytes 131072 | tf_op jit(solution)/shard_map/all_to_all | solution.py:80
  208.7 7.5 %all-to-all-done.1 = bf16[16,2,1024]{2,1,0:T(2,128)(2,1)S(1)} async-done(((bf16[16,2,1024]{2,1,0:T(2,128)(2,1)}), bf16[16,2,1024]{2,1,0:T(2,128)(2,1)S(1)}, u32[]{:S(2)}, u32[]{:S(2)}) %all-to-all-start.1) | async-done | bytes 65568 | tf_op jit(solution)/shard_map/all_to_all | solution.py:80
  216.3 1.9 all_gather.3
  218.2 10.3 %convolution_convert_fusion = bf16[128,16384]{1,0:T(8,128)(2,1)} fusion(bf16[16384,512]{1,0:T(8,128)(2,1)} %param.13, bf16[1,128,512]{2,1,0:T(8,128)(2,1)S(1)} %all_gather.3), kind=kOutput, calls=%fused_computation.6 | convolution fusion | flops 2149580800 | bytes 21102592 | tf_op jit(solution)/shard_map/skm,dm->skd/dot_general | solution.py:89
  228.6 6.4 %copy.40 = bf16[128,16384]{0,1:T(8,128)(2,1)} copy(bf16[128,16384]{1,0:T(8,128)(2,1)} %convolution_convert_fusion) | data formatting | bytes 8388608 | tf_op jit(solution)/shard_map/convert_element_type | solution.py:94
  235.0 3.8 %gather_fusion.3 = bf16[512,128]{1,0:T(8,128)(2,1)S(1)} fusion(bf16[128,16384]{0,1:T(8,128)(2,1)} %copy.40, s32[1024]{0:T(1024)S(1)} %pad_clamp_fusion), kind=kCustom, calls=%fused_computation.1.clone | custom fusion | bytes 264192 | tf_op jit(solution)/shard_map/jit(_take)/gather | solution.py:95
  238.9 1.0 collective-permute-start
  239.9 3.8 %gather_fusion.2 = bf16[512,128]{1,0:T(8,128)(2,1)S(1)} fusion(bf16[128,16384]{0,1:T(8,128)(2,1)} %copy.40, s32[1024]{0:T(1024)S(1)} %pad_clamp_fusion.1), kind=kCustom, calls=%fused_computation.clone | custom fusion | bytes 264192 | tf_op jit(solution)/shard_map/jit(_take)/gather | solution.py:96
  243.8 1.3 collective-permute-start.1
  245.2 0.7 convert_element_type.61
  245.8 6.8 %scatter_custom_fusion = bf16[128,16384]{0,1:T(8,128)(2,1)} fusion(bf16[128,16384]{0,1:T(8,128)(2,1)} %copy.40, s32[512]{0:T(512)S(1)} %compare_select_fusion.14, bf16[1,128,512]{1,2,0:T(8,128)(2,1)S(1)} %collective-permute-done, f32[]{:T(128)} %constant.134.clone.1, bf16[512,128]{1,0:T(8,128)(2,1)S(1)} %gather_fusion.2, ...), kind=kCustom, calls=%fused_computation.23 | custom fusion | flops 393216 | bytes 4457472 | tf_op jit(solution)/shard_map/scatter | solution.py:107
  253.0 6.8 %scatter_custom_fusion.1 = bf16[128,16384]{0,1:T(8,128)(2,1)} fusion(bf16[128,16384]{0,1:T(8,128)(2,1)} %scatter_custom_fusion, s32[512]{0:T(512)S(1)} %compare_select_fusion.13, bf16[1,128,512]{1,2,0:T(8,128)(2,1)S(1)} %collective-permute-done.1, f32[]{:T(128)} %constant.134.clone.1, bf16[512,128]{1,0:T(8,128)(2,1)S(1)} %gather_fusion.3, ...), kind=kCustom, calls=%fused_computation.25 | custom fusion | flops 393216 | bytes 4457472 | tf_op jit(solution)/shard_map/scatter | solution.py:107
  259.8 6.4 %copy.41 = bf16[1,128,16384]{2,1,0:T(8,128)(2,1)} copy(bf16[1,128,16384]{1,2,0:T(8,128)(2,1)} %bitcast.173) | data formatting | bytes 8388608
  (77 shorter events, 5.6 us)
Async XLA Ops:
  7.2 22.4 %copy-start = (f32[8,512]{1,0:T(8,128)S(1)}, f32[8,512]{1,0:T(8,128)}, u32[]{:S(2)}) copy-start(f32[8,512]{1,0:T(8,128)} %param.16) | copy-start | bytes 49156
  7.2 11.8 %copy-start.2 = (f32[64]{0:T(128)S(1)}, f32[64]{0:T(128)}, u32[]{:S(2)}) copy-start(f32[64]{0:T(128)} %param.19) | copy-start | bytes 772
  7.2 14.7 %copy-start.5 = (s32[512]{0:T(512)S(1)}, s32[512]{0:T(512)}, u32[]{:S(2)}) copy-start(s32[512]{0:T(512)} %param.21) | copy-start | bytes 6148
  7.2 15.4 %copy-start.6 = (s32[512]{0:T(512)S(1)}, s32[512]{0:T(512)}, u32[]{:S(2)}) copy-start(s32[512]{0:T(512)} %param.20) | copy-start | bytes 6148
  7.2 15.4 %copy-start.1 = (f32[512]{0:T(512)S(1)}, f32[512]{0:T(512)}, u32[]{:S(2)}) copy-start(f32[512]{0:T(512)} %param.18) | copy-start | bytes 6148
  7.2 26.9 %reduce-scatter.2.cloned.1.call-start = ((), (), s32[]{:S(2)}) async-start(), calls=%async_computation.3 | async-start | bytes 393216 | tf_op jit(solution)/shard_map/reduce_scatter | solution.py:45
  17.4 16.8 %copy-start.3 = (f32[1,128,256]{2,1,0:T(8,128)S(1)}, f32[1,128,256]{2,1,0:T(8,128)}, u32[]{:S(2)}) copy-start(f32[1,128,256]{2,1,0:T(8,128)} %param.14) | copy-start | bytes 393220
  122.1 16.6 %copy-start.4 = (f32[16,512]{1,0:T(8,128)S(1)}, f32[16,512]{1,0:T(8,128)}, u32[]{:S(2)}) copy-start(f32[16,512]{1,0:T(8,128)} %param.17) | copy-start | bytes 98308
  130.4 47.2 %all-to-all-start = ((f32[16,1,2048]{2,1,0:T(1,128)}), f32[16,1,2048]{2,1,0:T(1,128)S(1)}, u32[]{:S(2)}, u32[]{:S(2)}) async-start(f32[16,1,2048]{2,1,0:T(1,128)} %reshape.603), calls=%async_computation.1 | async-start | bytes 262144 | tf_op jit(solution)/shard_map/all_to_all | solution.py:58
  201.8 14.4 %all-to-all-start.1 = ((bf16[16,2,1024]{2,1,0:T(2,128)(2,1)}), bf16[16,2,1024]{2,1,0:T(2,128)(2,1)S(1)}, u32[]{:S(2)}, u32[]{:S(2)}) async-start(bf16[16,2,1024]{2,1,0:T(2,128)(2,1)} %copy.36), calls=%async_computation.2 | async-start | bytes 131072 | tf_op jit(solution)/shard_map/all_to_all | solution.py:80
  238.9 7.0 %collective-permute-start = (bf16[1,128,512]{1,2,0:T(8,128)(2,1)S(1)}, bf16[1,128,512]{1,2,0:T(8,128)(2,1)S(1)}, u32[]{:S(2)}, u32[]{:S(2)}) collective-permute-start(bf16[1,128,512]{1,2,0:T(8,128)(2,1)S(1)} %bitcast_select_fusion), channel_id=1, source_target_pairs={{0,30},{2,0},{4,2},{6,4},{8,6},{10,8},{12,10},{14,12},{16,14},{18,... | collective-permute-start | bytes 393224 | tf_op jit(solution)/shard_map/ppermute | solution.py:11
  243.8 9.1 %collective-permute-start.1 = (bf16[1,128,512]{1,2,0:T(8,128)(2,1)S(1)}, bf16[1,128,512]{1,2,0:T(8,128)(2,1)S(1)}, u32[]{:S(2)}, u32[]{:S(2)}) collective-permute-start(bf16[1,128,512]{1,2,0:T(8,128)(2,1)S(1)} %bitcast_select_fusion.1), channel_id=1, source_target_pairs={{0,2},{2,4},{4,6},{6,8},{8,10},{10,12},{12,14},{14,16},{16,18},{18... | collective-permute-start | bytes 393224 | tf_op jit(solution)/shard_map/ppermute | solution.py:11
Sparse Core Ops, SparseCore 0:
  17.5 10.4 reduce-scatter.1
where the time goes:
time: 274 us; the launch traced here: 273 us
  other arithmetic  133 us (49%)
  local copies, waits for them, and re-layouts  74.7 us (27%)
  matrix products  23.1 us (8%)
  starting transfers between devices  17.6 us (6%)
  between operations  15.1 us (6%)
  waiting for transfers between devices  7.83 us (3%)
    unnamed x1, other arithmetic  74.5 us
    select_n x1, other arithmetic, shards(): shifted = stiff - jnp.take(omega_sq, freq_idx)[None, :]  35.5 us
    unnamed x19, local copies, waits for them, and re-layouts  30 us
    scatter x2, other arithmetic, shards(): raw.at[:, :, iface_right].set(right_new).at[:, :, iface_left].set(left_new)  13.7 us
    reshape x2, local copies, waits for them, and re-layouts, shards(): (force - dev_rows[:, None, :] * response).reshape(local_sec, 2, width)  12.1 us
    dot_general x1, matrix products, shards(): jnp.einsum('skm,dm->skd', lax.all_gather(rounded, 'dof', axis=2, tiled=Tr...  10.3 us
    dot_general x1, matrix products, shards(): jnp.dot(loads.reshape(local_sec * rows_two, dof_rows), modes, preferred_e...  10.1 us
    all_to_all x1, starting transfers between devices, shards(): lax.all_to_all(rest, 'sector', split_axis=2, concat_axis=0, tiled=True)  8.35 us
  transfers between devices with their start and end apart: 5, of which 2 were waited for; matrix products, arithmetic and copies ran while one was open for 24% of the time, Pallas kernels for 0%

commit v1 on v0

v1 whole, which is shorter than its diff:
```python
import functools
import math

import jax
import jax.numpy as jnp
from jax import lax
from jax.experimental import pallas as pl
from jax.experimental.pallas import tpu as pltpu
from jax.sharding import PartitionSpec as P

MESH = pl.DeviceIdType.MESH
LANES = 128


def shifted_2(shard, axis, by):
    size = lax.axis_size(axis)
    return lax.ppermute(shard, axis, [(i, (i + by) % size) for i in range(size)])


def transform(re, im, sign):
    n = len(re)
    if n == 1:
        return re, im
    if n % 2:
        out_re, out_im = [], []
        for h in range(n):
            sum_re, sum_im = re[0], im[0]
            for s in range(1, n):
                turn = 2.0 * math.pi * ((h * s) % n) / n
                cosine, sine = math.cos(turn), sign * math.sin(turn)
                sum_re = sum_re + re[s] * cosine - im[s] * sine
                sum_im = sum_im + im[s] * cosine + re[s] * sine
            out_re.append(sum_re)
            out_im.append(sum_im)
        return out_re, out_im
    even_re, even_im = transform(re[0::2], im[0::2], sign)
    odd_re, odd_im = transform(re[1::2], im[1::2], sign)
    half = n // 2
    out_re, out_im = [None] * n, [None] * n
    for k in range(half):
        if k == 0:
            turned_re, turned_im = odd_re[k], odd_im[k]
        elif 4 * k == n:
            turned_re, turned_im = -sign * odd_im[k], sign * odd_re[k]
        else:
            cosine = math.cos(2.0 * math.pi * k / n)
            sine = sign * math.sin(2.0 * math.pi * k / n)
            turned_re = odd_re[k] * cosine - odd_im[k] * sine
            turned_im = odd_re[k] * sine + odd_im[k] * cosine
        out_re[k], out_im[k] = even_re[k] + turned_re, even_im[k] + turned_im
        out_re[k + half] = even_re[k] - turned_re
        out_im[k + half] = even_im[k] - turned_im
    return out_re, out_im


def modal_kernel(
    nsec, ndof, steps,
    loads_ref, modes_ref, resp_ref, pattern_ref, dev_ref, eigen_ref, loss_ref, omega_ref,
    mine_ref, full_ref,
    acc, send_a, recv_a, send_b, recv_b, coef, sa, ra, sb, rb,
):
    step = pl.program_id(0)
    sec, dof = lax.axis_index("sector"), lax.axis_index("dof")
    count = nsec * ndof
    me = sec * ndof + dof
    rows, modes_all = acc.shape
    freqs, half = rows // 2, modes_all // ndof
    groups, share = half // LANES, freqs // nsec
    part = groups * share
    barrier = pltpu.get_barrier_semaphore()

    def peer(k):
        return lax.rem(me + k, count)

    def place(device):
        return {"sector": device // ndof, "dof": lax.rem(device, ndof)}

    @pl.when(step == 0)
    def _():
        acc[...] = jnp.zeros_like(acc)

        def greet(k, carry):
            pl.semaphore_signal(barrier, inc=1, device_id=place(peer(k)), device_id_type=MESH)
            return carry

        lax.fori_loop(1, count, greet, 0)

    acc[...] += jnp.dot(loads_ref[...], modes_ref[...], preferred_element_type=jnp.float32)

    def pick(values):
        total = None
        for d in range(ndof):
            term = jnp.where(dof == d, values[:, d * half : (d + 1) * half], 0.0)
            total = term if total is None else total + term
        return total

    def pieces():
        for kind in range(2):
            for g in range(groups):
                yield kind, g, (kind * groups + g) * share

    @pl.when(step == steps - 1)
    def _():
        table = dev_ref[...]
        chosen = lax.broadcasted_iota(jnp.int32, table.shape, 0) == pattern_ref[0]
        dev_row = pick(jnp.sum(jnp.where(chosen, table, 0.0), axis=0, keepdims=True))
        scaled = dev_row * resp_ref[...]
        for d in range(ndof):
            cols = slice(d * half, (d + 1) * half)
            acc[:, cols] = acc[:, cols] - jnp.where(dof == d, scaled, 0.0)
        for t in range(nsec):
            for d in range(ndof):
                parts = []
                for kind, g, _ in pieces():
                    first = kind * freqs + t * share
                    left = d * half + g * LANES
                    parts.append(acc[first : first + share, left : left + LANES])
                send_a[t * ndof + d] = jnp.concatenate(parts, 0).astype(jnp.bfloat16)
        pl.semaphore_wait(barrier, count - 1)

        def copy_a(to, origin):
            return pltpu.make_async_remote_copy(
                src_ref=send_a.at[to], dst_ref=recv_a.at[origin],
                send_sem=sa.at[to], recv_sem=ra.at[origin],
                device_id=place(to), device_id_type=MESH,
            )

        def copy_b(to, origin):
            return pltpu.make_async_remote_copy(
                src_ref=send_b.at[to // ndof], dst_ref=recv_b.at[origin],
                send_sem=sb.at[to], recv_sem=rb.at[origin],
                device_id=place(to), device_id_type=MESH,
            )

        def start_a(k, carry):
            copy_a(peer(k), me).start()
            return carry

        lax.fori_loop(1, count, start_a, 0)
        recv_a[pl.ds(me, 1)] = send_a[pl.ds(me, 1)]

        row = lax.rem(lax.broadcasted_iota(jnp.int32, (part, LANES), 0), share)
        omega = jnp.zeros((part, LANES), jnp.float32)
        for j in range(share):
            omega = jnp.where(row == j, omega_ref[sec * share + j], omega)

        def spread(line):
            line = pick(line)
            return jnp.concatenate(
                [
                    jnp.broadcast_to(line[:, g * LANES : (g + 1) * LANES], (share, LANES))
                    for g in range(groups)
                ],
                0,
            )

        loss = spread(loss_ref[...])
        for h in range(nsec):
            stiff = spread(eigen_ref[h : h + 1, :])
            shifted, damped = stiff - omega, loss * stiff
            denom = shifted * shifted + damped * damped
            coef[0, h] = shifted / denom
            coef[1, h] = damped / denom

        def wait_a(k, carry):
            copy_a(peer(k), peer(k)).wait_recv()
            return carry

        lax.fori_loop(1, count, wait_a, 0)
        rest_re, rest_im = [], []
        for s in range(nsec):
            block = recv_a[s * ndof].astype(jnp.float32)
            for d in range(1, ndof):
                block = block + recv_a[s * ndof + d].astype(jnp.float32)
            rest_re.append(block[:part])
            rest_im.append(block[part:])
        spec_re, spec_im = transform(rest_re, rest_im, -1.0)
        solved_re, solved_im = [], []
        for h in range(nsec):
            a, b = coef[0, h], coef[1, h]
            solved_re.append(spec_re[h] * a + spec_im[h] * b)
            solved_im.append(spec_im[h] * a - spec_re[h] * b)
        out_re, out_im = transform(solved_re, solved_im, 1.0)
        for s in range(nsec):
            block = jnp.concatenate([out_re[s], out_im[s]], 0) * (1.0 / nsec)
            send_b[s] = block.astype(jnp.bfloat16)

        def start_b(k, carry):
            copy_b(peer(k), me).start()
            return carry

        lax.fori_loop(1, count, start_b, 0)
        recv_b[pl.ds(me, 1)] = send_b[pl.ds(sec, 1)]

        def wait_b(k, carry):
            copy_b(peer(k), peer(k)).wait_recv()
            return carry

        lax.fori_loop(1, count, wait_b, 0)
        for t in range(nsec):
            for d in range(ndof):
                block = recv_b[t * ndof + d].astype(jnp.float32)
                for kind, g, at in pieces():
                    first = kind * freqs + t * share
                    left = d * half + g * LANES
                    acc[first : first + share, left : left + LANES] = block[at : at + share]
        whole = acc[...]
        full_ref[...] = whole.astype(jnp.bfloat16)
        mine_ref[...] = pick(whole)

        def sent(k, carry):
            copy_a(peer(k), me).wait_send()
            copy_b(peer(k), me).wait_send()
            return carry

        lax.fori_loop(1, count, sent, 0)


def modal_solve(loads, modes, response, pattern, deviation, eigen, loss, omega_sq):
    rows, depth = loads.shape
    modes_all = modes.shape[1]
    nsec, ndof = lax.axis_size("sector"), lax.axis_size("dof")
    half = modes_all // ndof
    count = nsec * ndof
    part = (half // LANES) * (rows // 2 // nsec)
    tile = min(depth, 2048)
    steps = depth // tile

    def still(shape):
        return pl.BlockSpec(shape, lambda k: (0,) * len(shape))

    smem = pl.BlockSpec(memory_space=pltpu.SMEM)
    block = (2 * part, LANES)
    return pl.pallas_call(
        functools.partial(modal_kernel, nsec, ndof, steps),
        grid=(steps,),
        out_shape=(
            jax.ShapeDtypeStruct((rows, half), jnp.float32),
            jax.ShapeDtypeStruct((rows, modes_all), jnp.bfloat16),
        ),
        in_specs=[
            pl.BlockSpec((rows, tile), lambda k: (0, k)),
            pl.BlockSpec((tile, modes_all), lambda k: (k, 0)),
            still(response.shape),
            smem,
            still(deviation.shape),
            still(eigen.shape),
            still((1, modes_all)),
            smem,
        ],
        out_specs=(still((rows, half)), still((rows, modes_all))),
        scratch_shapes=[
            pltpu.VMEM((rows, modes_all), jnp.float32),
            pltpu.VMEM((count,) + block, jnp.bfloat16),
            pltpu.VMEM((count,) + block, jnp.bfloat16),
            pltpu.VMEM((nsec,) + block, jnp.bfloat16),
            pltpu.VMEM((count,) + block, jnp.bfloat16),
            pltpu.VMEM((2, nsec, part, LANES), jnp.float32),
            pltpu.SemaphoreType.DMA((count,)),
            pltpu.SemaphoreType.DMA((count,)),
            pltpu.SemaphoreType.DMA((count,)),
            pltpu.SemaphoreType.DMA((count,)),
        ],
        compiler_params=pltpu.CompilerParams(
            dimension_semantics=("arbitrary",), collective_id=0, has_side_effects=True
        ),
        name="modal_solve",
    )(loads, modes, response, pattern, deviation, eigen, loss.reshape(1, modes_all), omega_sq)


def shards(
    loads, modes, response, pattern, deviation, eigen, loss, omega_sq, iface_left, iface_right
):
    mine, full = modal_solve(
        loads[0], modes, response[0], pattern, deviation, eigen, loss, omega_sq
    )
    modal_response = mine[None]
    raw = jnp.einsum(
        "skm,dm->skd", full[None], modes, preferred_element_type=jnp.float32
    ).astype(jnp.bfloat16)
    left_vals = jnp.take(raw, iface_left, axis=2)
    right_vals = jnp.take(raw, iface_right, axis=2)
    next_left = shifted_2(left_vals, "sector", -1)
    prev_right = shifted_2(right_vals, "sector", 1)
    left_after = next_left
    right_before = prev_right
    right_new = (0.5 * (right_vals.astype(jnp.float32) + left_after.astype(jnp.float32))).astype(
        jnp.bfloat16
    )
    left_new = (0.5 * (right_before.astype(jnp.float32) + left_vals.astype(jnp.float32))).astype(
        jnp.bfloat16
    )
    displacement = raw.at[:, :, iface_right].set(right_new).at[:, :, iface_left].set(left_new)
    return (modal_response, displacement)


def solution(mesh):
    placed = (
        P("sector", None, "dof"),
        P("dof", None),
        P("sector", None, "dof"),
        P("sector"),
        P(),
        P(),
        P(),
        P(),
        P("dof"),
        P("dof"),
    )
    return jax.shard_map(
        shards,
        mesh=mesh,
        in_specs=placed,
        out_specs=(P("sector", None, "dof"), P("sector", None, "dof")),
        check_vma=False,
    )
```

time: 274 us -> 82.3 us (0.30)
  other arithmetic: 133 us -> 15.4 us
  local copies, waits for them, and re-layouts: 74.7 us -> 21 us
  Pallas kernels: 0 us -> 26.3 us
  between operations: 15.1 us -> 1.35 us
  matrix products: 23.1 us -> 10.4 us
  starting transfers between devices: 17.6 us -> 5.25 us
  waiting for transfers between devices: 7.83 us -> 1.96 us
    unnamed x1 -> x0, other arithmetic: 74.5 us -> none
    select_n x4 -> x0, other arithmetic: 35.6 us -> none  [the longest x1 35.5 us: shards(): shifted = stiff - jnp.take(omega_sq, freq_idx)[None, :]]
    pallas_call x0 -> x1, Pallas kernels: none -> 26.3 us  [modal_solve(): pl.pallas_call(functools.partial(modal_kernel, nsec, ndof, steps), grid=(...]
    unnamed x19 -> x6, local copies, waits for them, and re-layouts: 30 us -> 7.06 us
    all_to_all x2 -> x0, starting transfers between devices: 15.3 us -> none  [the longest x1 8.35 us: shards(): lax.all_to_all(rest, 'sector', split_axis=2, concat_axis=0, tiled=True)]
    gather x7 -> x0, local copies, waits for them, and re-layouts: 12.7 us -> none  [the longest x1 6.87 us: shards(): damped = jnp.take(loss, mode_idx)[None, :] * stiff]
    dot_general x11 -> x1, matrix products: 23.1 us -> 10.4 us  [shards(): jnp.einsum('skm,dm->skd', full[None], modes, preferred_element_type=jnp.f...]
    reshape x2 -> x0, local copies, waits for them, and re-layouts: 12.1 us -> none  [shards(): (force - dev_rows[:, None, :] * response).reshape(local_sec, 2, width)]
  transfers between devices with their start and end apart: 5 -> 2, of which waited for: 2 -> 1; matrix products, arithmetic and copies ran while one was open for 24% -> 13% of each run, Pallas kernels for 0% -> 0%
where the time goes in v1:
time: 82.3 us; the launch traced here: 81.6 us
  Pallas kernels  26.3 us (32%)
  local copies, waits for them, and re-layouts  21 us (26%)
  other arithmetic  15.4 us (19%)
  matrix products  10.4 us (13%)
  starting transfers between devices  5.25 us (6%)
  waiting for transfers between devices  1.96 us (2%)
  between operations  1.35 us (2%)
    pallas_call x1, Pallas kernels, modal_solve(): pl.pallas_call(functools.partial(modal_kernel, nsec, ndof, steps), grid=(...  26.3 us
    scatter x2, other arithmetic, shards(): raw.at[:, :, iface_right].set(right_new).at[:, :, iface_left].set(left_new)  13.7 us
    dot_general x1, matrix products, shards(): jnp.einsum('skm,dm->skd', full[None], modes, preferred_element_type=jnp.f...  10.4 us
    unnamed x6, local copies, waits for them, and re-layouts  7.06 us
    convert_element_type x1, local copies, waits for them, and re-layouts, shards(): raw = jnp.einsum('skm,dm->skd', full[None], modes, preferred_element_type...  6.39 us
    ppermute x2, starting transfers between devices, shifted_2(): lax.ppermute(shard, axis, [(i, (i + by) % size) for i in range(size)])  5.25 us
    gather x1, local copies, waits for them, and re-layouts, shards(): right_vals = jnp.take(raw, iface_right, axis=2)  3.78 us
    gather x1, local copies, waits for them, and re-layouts, shards(): left_vals = jnp.take(raw, iface_left, axis=2)  3.78 us
  transfers between devices with their start and end apart: 2, of which 1 were waited for; matrix products, arithmetic and copies ran while one was open for 13% of the time, Pallas kernels for 0%

profile of v1, /device:TPU:0, one launch (start us, length us, event | category | flops | bytes accessed | tf_op | source)
XLA Modules:
  0.0 81.6 jit_solution(1643297147565139480)
XLA Ops:
  0.6 0.7 compare_select_fusion
  1.3 0.7 compare_and_fusion
  2.7 26.3 %modal_solve.1 = (f32[128,256]{1,0:T(8,128)}, bf16[128,512]{1,0:T(8,128)(2,1)}) custom-call(bf16[128,16384]{1,0:T(8,128)(2,1)} %bitcast.33, bf16[16384,512]{1,0:T(8,128)(2,1)} %modes_ref.1, f32[128,256]{1,0:T(8,128)} %bitcast.34, s32[1]{0:T(128)S(6)} %copy.19.pattern_ref, f32[8,512]{1,0:T(8,128)} %dev_ref.1, f32[16,512]{1,0:T(8,128)} %eigen_ref.1, ...), custom_call_target="tpu_custom_call" | custom-call | tf_op jit(solution)/shard_map/modal_solve/pallas_call | solution.py:234
  29.0 10.4 %convolution_convert_fusion = bf16[128,16384]{1,0:T(8,128)(2,1)} fusion(bf16[128,512]{1,0:T(8,128)(2,1)} %get-tuple-element.6, bf16[16384,512]{1,0:T(8,128)(2,1)} %modes_ref.1), kind=kOutput, calls=%fused_computation.4 | convolution fusion | flops 2149580800 | bytes 21102592 | tf_op jit(solution)/shard_map/skm,dm->skd/dot_general | solution.py:278
  39.4 0.0 copy-start.1
  39.4 6.4 %copy.14 = bf16[128,16384]{0,1:T(8,128)(2,1)} copy(bf16[128,16384]{1,0:T(8,128)(2,1)} %convolution_convert_fusion) | data formatting | bytes 8388608 | tf_op jit(solution)/shard_map/convert_element_type | solution.py:280
  45.8 3.8 %gather_fusion.1 = bf16[512,128]{1,0:T(8,128)(2,1)S(1)} fusion(bf16[128,16384]{0,1:T(8,128)(2,1)} %copy.14, s32[1024]{0:T(1024)S(1)} %pad_clamp_fusion), kind=kCustom, calls=%fused_computation.1.clone | custom fusion | bytes 264192 | tf_op jit(solution)/shard_map/jit(_take)/gather | solution.py:281
  49.5 0.1 bitcast_select_fusion
  49.7 5.2 %collective-permute-start = (bf16[1,128,512]{1,2,0:T(8,128)(2,1)S(1)}, bf16[1,128,512]{1,2,0:T(8,128)(2,1)S(1)}, u32[]{:S(2)}, u32[]{:S(2)}) collective-permute-start(bf16[1,128,512]{1,2,0:T(8,128)(2,1)S(1)} %bitcast_select_fusion), channel_id=1, source_target_pairs={{0,30},{2,0},{4,2},{6,4},{8,6},{10,8},{12,10},{14,12},{16,14},{18,... | collective-permute-start | bytes 393224 | tf_op jit(solution)/shard_map/ppermute | solution.py:17
  54.9 0.0 copy-done.1
  54.9 3.8 %gather_fusion = bf16[512,128]{1,0:T(8,128)(2,1)S(1)} fusion(bf16[128,16384]{0,1:T(8,128)(2,1)} %copy.14, s32[1024]{0:T(1024)S(1)} %pad_clamp_fusion.1), kind=kCustom, calls=%fused_computation.clone | custom fusion | bytes 264192 | tf_op jit(solution)/shard_map/jit(_take)/gather | solution.py:282
  58.7 0.1 bitcast_select_fusion.1
  58.8 0.1 collective-permute-start.1
  58.9 0.0 collective-permute-done
  58.9 6.9 %scatter_custom_fusion = bf16[128,16384]{0,1:T(8,128)(2,1)} fusion(bf16[128,16384]{0,1:T(8,128)(2,1)} %copy.14, s32[512]{0:T(512)S(1)} %compare_select_fusion.1, bf16[1,128,512]{1,2,0:T(8,128)(2,1)S(1)} %collective-permute-done, f32[]{:T(128)} %constant.3.clone.1, bf16[512,128]{1,0:T(8,128)(2,1)S(1)} %gather_fusion, pred[512]{0:T(512)(128)(4,1)S(1)} %compare_and_fusion.1), kind=kCustom, calls=%fused_computation.8 | custom fusion | flops 393216 | bytes 4457472 | tf_op jit(solution)/shard_map/scatter | solution.py:293
  65.8 2.0 %collective-permute-done.1 = bf16[1,128,512]{1,2,0:T(8,128)(2,1)S(1)} collective-permute-done((bf16[1,128,512]{1,2,0:T(8,128)(2,1)S(1)}, bf16[1,128,512]{1,2,0:T(8,128)(2,1)S(1)}, u32[]{:S(2)}, u32[]{:S(2)}) %collective-permute-start.1) | collective-permute-done | bytes 131104 | tf_op jit(solution)/shard_map/ppermute | solution.py:17
  67.7 6.8 %scatter_custom_fusion.1 = bf16[128,16384]{0,1:T(8,128)(2,1)} fusion(bf16[128,16384]{0,1:T(8,128)(2,1)} %scatter_custom_fusion, s32[512]{0:T(512)S(1)} %compare_select_fusion, bf16[1,128,512]{1,2,0:T(8,128)(2,1)S(1)} %collective-permute-done.1, f32[]{:T(128)} %constant.3.clone.1, bf16[512,128]{1,0:T(8,128)(2,1)S(1)} %gather_fusion.1, ...), kind=kCustom, calls=%fused_computation.10 | custom fusion | flops 393216 | bytes 4457472 | tf_op jit(solution)/shard_map/scatter | solution.py:293
  74.6 0.0 copy-start
  74.6 6.4 %copy.15 = bf16[1,128,16384]{2,1,0:T(8,128)(2,1)} copy(bf16[1,128,16384]{1,2,0:T(8,128)(2,1)} %bitcast.32) | data formatting | bytes 8388608
  81.0 0.0 copy-done
  81.0 0.7 copy.20
  (4 shorter events, 0.0 us)
Async XLA Ops:
  39.4 15.5 %copy-start.1 = (s32[512]{0:T(512)S(1)}, s32[512]{0:T(512)}, u32[]{:S(2)}) copy-start(s32[512]{0:T(512)} %param.21) | copy-start | bytes 6148
  49.7 9.2 %collective-permute-start = (bf16[1,128,512]{1,2,0:T(8,128)(2,1)S(1)}, bf16[1,128,512]{1,2,0:T(8,128)(2,1)S(1)}, u32[]{:S(2)}, u32[]{:S(2)}) collective-permute-start(bf16[1,128,512]{1,2,0:T(8,128)(2,1)S(1)} %bitcast_select_fusion), channel_id=1, source_target_pairs={{0,30},{2,0},{4,2},{6,4},{8,6},{10,8},{12,10},{14,12},{16,14},{18,... | collective-permute-start | bytes 393224 | tf_op jit(solution)/shard_map/ppermute | solution.py:17
  58.8 8.9 %collective-permute-start.1 = (bf16[1,128,512]{1,2,0:T(8,128)(2,1)S(1)}, bf16[1,128,512]{1,2,0:T(8,128)(2,1)S(1)}, u32[]{:S(2)}, u32[]{:S(2)}) collective-permute-start(bf16[1,128,512]{1,2,0:T(8,128)(2,1)S(1)} %bitcast_select_fusion.1), channel_id=1, source_target_pairs={{0,2},{2,4},{4,6},{6,8},{8,10},{10,12},{12,14},{14,16},{16,18},{18... | collective-permute-start | bytes 393224 | tf_op jit(solution)/shard_map/ppermute | solution.py:17
  74.6 6.4 %copy-start = (f32[128,256]{1,0:T(8,128)S(1)}, f32[128,256]{1,0:T(8,128)}, u32[]{:S(2)}) copy-start(f32[128,256]{1,0:T(8,128)} %get-tuple-element.5) | copy-start | bytes 393220

commit v2 on v1

--- a/solution.py
+++ b/solution.py
@@ -10,11 +10,6 @@
 
 MESH = pl.DeviceIdType.MESH
 LANES = 128
-
-
-def shifted_2(shard, axis, by):
-    size = lax.axis_size(axis)
-    return lax.ppermute(shard, axis, [(i, (i + by) % size) for i in range(size)])
 
 
 def transform(re, im, sign):
@@ -56,8 +51,8 @@
 def modal_kernel(
     nsec, ndof, steps,
     loads_ref, modes_ref, resp_ref, pattern_ref, dev_ref, eigen_ref, loss_ref, omega_ref,
-    mine_ref, full_ref,
-    acc, send_a, recv_a, send_b, recv_b, coef, sa, ra, sb, rb,
+    mine_ref, three_ref,
+    acc, send_a, recv_a, send_b, recv_b, coef, own, near, sa, ra, sb, rb, sc, rc,
 ):
     step = pl.program_id(0)
     sec, dof = lax.axis_index("sector"), lax.axis_index("dof")
@@ -204,9 +199,20 @@
                     first = kind * freqs + t * share
                     left = d * half + g * LANES
                     acc[first : first + share, left : left + LANES] = block[at : at + share]
-        whole = acc[...]
-        full_ref[...] = whole.astype(jnp.bfloat16)
-        mine_ref[...] = pick(whole)
+        own[...] = acc[...].astype(jnp.bfloat16)
+
+        def copy_c(side):
+            to = lax.rem(sec + (nsec - 1, 1)[side], nsec)
+            return pltpu.make_async_remote_copy(
+                src_ref=own, dst_ref=near.at[side],
+                send_sem=sc.at[side], recv_sem=rc.at[side],
+                device_id={"sector": to, "dof": dof}, device_id_type=MESH,
+            )
+
+        for side in range(2):
+            copy_c(side).start()
+        mine_ref[...] = pick(acc[...])
+        three_ref[:rows] = own[...]
 
         def sent(k, carry):
             copy_a(peer(k), me).wait_send()
@@ -214,6 +220,9 @@
             return carry
 
         lax.fori_loop(1, count, sent, 0)
+        for side in range(2):
+            copy_c(side).wait()
+            three_ref[(side + 1) * rows : (side + 2) * rows] = near[side]
 
 
 def modal_solve(loads, modes, response, pattern, deviation, eigen, loss, omega_sq):
@@ -236,7 +245,7 @@
         grid=(steps,),
         out_shape=(
             jax.ShapeDtypeStruct((rows, half), jnp.float32),
-            jax.ShapeDtypeStruct((rows, modes_all), jnp.bfloat16),
+            jax.ShapeDtypeStruct((3 * rows, modes_all), jnp.bfloat16),
         ),
         in_specs=[
             pl.BlockSpec((rows, tile), lambda k: (0, k)),
@@ -248,7 +257,7 @@
             still((1, modes_all)),
             smem,
         ],
-        out_specs=(still((rows, half)), still((rows, modes_all))),
+        out_specs=(still((rows, half)), still((3 * rows, modes_all))),
         scratch_shapes=[
             pltpu.VMEM((rows, modes_all), jnp.float32),
             pltpu.VMEM((count,) + block, jnp.bfloat16),
@@ -256,10 +265,14 @@
             pltpu.VMEM((nsec,) + block, jnp.bfloat16),
             pltpu.VMEM((count,) + block, jnp.bfloat16),
             pltpu.VMEM((2, nsec, part, LANES), jnp.float32),
+            pltpu.VMEM((rows, modes_all), jnp.bfloat16),
+            pltpu.VMEM((2, rows, modes_all), jnp.bfloat16),
             pltpu.SemaphoreType.DMA((count,)),
             pltpu.SemaphoreType.DMA((count,)),
             pltpu.SemaphoreType.DMA((count,)),
             pltpu.SemaphoreType.DMA((count,)),
+            pltpu.SemaphoreType.DMA((2,)),
+            pltpu.SemaphoreType.DMA((2,)),
         ],
         compiler_params=pltpu.CompilerParams(
             dimension_semantics=("arbitrary",), collective_id=0, has_side_effects=True
@@ -268,30 +281,86 @@
     )(loads, modes, response, pattern, deviation, eigen, loss.reshape(1, modes_all), omega_sq)
 
 
+def recover_kernel(
+    steps, three_ref, modes_ref, left_ref, right_ref, out_ref, here, after, before
+):
+    step = pl.program_id(0)
+    rows = out_ref.shape[0]
+    tile, wide = modes_ref.shape[0], out_ref.shape[1]
+    contract = (((1,), (1,)), ((), ()))
+
+    @pl.when(step < steps)
+    def _():
+        found = lax.dot_general(
+            modes_ref[...], three_ref[...], contract, preferred_element_type=jnp.float32
+        )
+        span = pl.ds(pl.multiple_of(step * tile, tile), tile)
+        here[span, :] = found[:, :rows]
+        after[span, :] = found[:, rows : 2 * rows]
+        before[span, :] = found[:, 2 * rows :]
+
+    @pl.when(step == steps - 1)
+    def _():
+        entries = left_ref.shape[0]
+        group = math.gcd(entries, 8)
+
+        def blend(block, carry):
+            new = []
+            for j in range(group):
+                left, right = left_ref[block * group + j], right_ref[block * group + j]
+                new.append((right, here[pl.ds(right, 1), :] + after[pl.ds(left, 1), :]))
+                new.append((left, before[pl.ds(right, 1), :] + here[pl.ds(left, 1), :]))
+            for at, value in new:
+                here[pl.ds(at, 1), :] = 0.5 * value
+            return carry
+
+        lax.fori_loop(0, entries // group, blend, 0)
+
+    @pl.when(step >= steps)
+    def _():
+        span = pl.ds(pl.multiple_of((step - steps) * wide, wide), wide)
+        shape = (rows, rows)
+        same = lax.broadcasted_iota(jnp.int32, shape, 0) == lax.broadcasted_iota(
+            jnp.int32, shape, 1
+        )
+        eye = jnp.where(same, 1.0, 0.0).astype(jnp.bfloat16)
+        out_ref[...] = lax.dot_general(
+            eye, here[span, :].astype(jnp.bfloat16), contract, preferred_element_type=jnp.float32
+        ).astype(jnp.bfloat16)
+
+
+def recover(three, modes, left, right):
+    depth, modes_all = modes.shape
+    rows = three.shape[0] // 3
+    tile, wide = min(depth, 1024), min(depth, 2048)
+    steps = depth // tile
+    smem = pl.BlockSpec(memory_space=pltpu.SMEM)
+    return pl.pallas_call(
+        functools.partial(recover_kernel, steps),
+        grid=(steps + depth // wide,),
+        out_shape=jax.ShapeDtypeStruct((rows, depth), jnp.bfloat16),
+        in_specs=[
+            pl.BlockSpec(three.shape, lambda k: (0, 0)),
+            pl.BlockSpec((tile, modes_all), lambda k: (jnp.minimum(k, steps - 1), 0)),
+            smem,
+            smem,
+        ],
+        out_specs=pl.BlockSpec((rows, wide), lambda k: (0, jnp.maximum(k - steps, 0))),
+        scratch_shapes=[pltpu.VMEM((depth, rows), jnp.float32)] * 3,
+        compiler_params=pltpu.CompilerParams(
+            dimension_semantics=("arbitrary",), vmem_limit_bytes=60 * 1024 * 1024
+        ),
+        name="recover",
+    )(three, modes, left, right)
+
+
 def shards(
     loads, modes, response, pattern, deviation, eigen, loss, omega_sq, iface_left, iface_right
 ):
-    mine, full = modal_solve(
+    mine, three = modal_solve(
         loads[0], modes, response[0], pattern, deviation, eigen, loss, omega_sq
     )
-    modal_response = mine[None]
-    raw = jnp.einsum(
-        "skm,dm->skd", full[None], modes, preferred_element_type=jnp.float32
-    ).astype(jnp.bfloat16)
-    left_vals = jnp.take(raw, iface_left, axis=2)
-    right_vals = jnp.take(raw, iface_right, axis=2)
-    next_left = shifted_2(left_vals, "sector", -1)
-    prev_right = shifted_2(right_vals, "sector", 1)
-    left_after = next_left
-    right_before = prev_right
-    right_new = (0.5 * (right_vals.astype(jnp.float32) + left_after.astype(jnp.float32))).astype(
-        jnp.bfloat16
-    )
-    left_new = (0.5 * (right_before.astype(jnp.float32) + left_vals.astype(jnp.float32))).astype(
-        jnp.bfloat16
-    )
-    displacement = raw.at[:, :, iface_right].set(right_new).at[:, :, iface_left].set(left_new)
-    return (modal_response, displacement)
+    return mine[None], recover(three, modes, iface_left, iface_right)[None]
 
 
 def solution(mesh):

time: 82.3 us -> 61.6 us (0.75)
  Pallas kernels: 26.3 us -> 59.1 us
  local copies, waits for them, and re-layouts: 21 us -> 0.66 us
  other arithmetic: 15.4 us -> 0 us
  matrix products: 10.4 us -> 0 us
  starting transfers between devices: 5.25 us -> 0 us
  waiting for transfers between devices: 1.96 us -> 0 us
    pallas_call x0 -> x1, Pallas kernels: none -> 24 us  [recover(): pl.pallas_call(functools.partial(recover_kernel, steps), grid=(steps + de...]
    scatter x2 -> x0, other arithmetic: 13.7 us -> none  [shards(): raw.at[:, :, iface_right].set(right_new).at[:, :, iface_left].set(left_new)]
    dot_general x1 -> x0, matrix products: 10.4 us -> none  [shards(): jnp.einsum('skm,dm->skd', full[None], modes, preferred_element_type=jnp.f...]
    pallas_call x1, Pallas kernels: 26.3 us -> 35.2 us  [modal_solve(): pl.pallas_call(functools.partial(modal_kernel, nsec, ndof, steps), grid=(...]
    gather x2 -> x0, local copies, waits for them, and re-layouts: 7.56 us -> none  [the longest x1 3.78 us: shards(): right_vals = jnp.take(raw, iface_right, axis=2)]
    unnamed x6 -> x3, local copies, waits for them, and re-layouts: 7.06 us -> 0.66 us
    convert_element_type x1 -> x0, local copies, waits for them, and re-layouts: 6.39 us -> none  [shards(): raw = jnp.einsum('skm,dm->skd', full[None], modes, preferred_element_type...]
    ppermute x2 -> x0, starting transfers between devices: 5.25 us -> none  [shifted_2(): lax.ppermute(shard, axis, [(i, (i + by) % size) for i in range(size)])]
  transfers between devices with their start and end apart: 2 -> 0, of which waited for: 1 -> 0; matrix products, arithmetic and copies ran while one was open for 13% -> 0% of each run, Pallas kernels for 0% -> 0%
where the time goes in v2:
time: 61.6 us; the launch traced here: 61.1 us
  Pallas kernels  59.1 us (96%)
  between operations  1.29 us (2%)
  local copies, waits for them, and re-layouts  0.66 us (1%)
    pallas_call x1, Pallas kernels, modal_solve(): pl.pallas_call(functools.partial(modal_kernel, nsec, ndof, steps), grid=(...  35.2 us
    pallas_call x1, Pallas kernels, recover(): pl.pallas_call(functools.partial(recover_kernel, steps), grid=(steps + de...  24 us

profile of v2, /device:TPU:0, one launch (start us, length us, event | category | flops | bytes accessed | tf_op | source)
XLA Modules:
  0.0 61.1 jit_solution(4566046418262444991)
XLA Ops:
  1.3 35.2 %modal_solve.1 = (f32[128,256]{1,0:T(8,128)}, bf16[384,512]{1,0:T(8,128)(2,1)}) custom-call(bf16[128,16384]{1,0:T(8,128)(2,1)} %bitcast.5, bf16[16384,512]{1,0:T(8,128)(2,1)} %modes_ref.3, f32[128,256]{1,0:T(8,128)} %bitcast.7, s32[1]{0:T(128)S(6)} %copy.13.pattern_ref, f32[8,512]{1,0:T(8,128)} %dev_ref.1, f32[16,512]{1,0:T(8,128)} %eigen_ref.1, ...), custom_call_target="tpu_custom_call" | custom-call | tf_op jit(solution)/shard_map/modal_solve/pallas_call | solution.py:243
  36.4 0.0 copy-start
  36.4 24.0 %recover.1 = bf16[128,16384]{1,0:T(8,128)(2,1)} custom-call(bf16[384,512]{1,0:T(8,128)(2,1)} %get-tuple-element.5.three_ref, bf16[16384,512]{1,0:T(8,128)(2,1)} %modes_ref.3, s32[512]{0:T(512)} %left_ref.1, s32[512]{0:T(512)} %right_ref.1), custom_call_target="tpu_custom_call" | custom-call | tf_op jit(solution)/shard_map/recover/pallas_call | solution.py:338
  60.4 0.0 copy-done
  60.4 0.7 %copy.14 = f32[1,128,256]{2,1,0:T(8,128)} copy(f32[1,128,256]{2,1,0:T(8,128)S(1)} %bitcast.8) | data formatting | bytes 262144
Async XLA Ops:
  36.4 24.0 %copy-start = (f32[128,256]{1,0:T(8,128)S(1)}, f32[128,256]{1,0:T(8,128)}, u32[]{:S(2)}) copy-start(f32[128,256]{1,0:T(8,128)} %get-tuple-element.4) | copy-start | bytes 393220

commit v3 on v1

v3 whole, which is shorter than its diff:
```python
import functools
import math

import jax
import jax.numpy as jnp
from jax import lax
from jax.experimental import pallas as pl
from jax.experimental.pallas import tpu as pltpu
from jax.sharding import PartitionSpec as P

MESH = pl.DeviceIdType.MESH
LANES = 128
LIMIT = 50 * 1024 * 1024


def transform(re, im, sign):
    n = len(re)
    if n == 1:
        return re, im
    if n % 2:
        out_re, out_im = [], []
        for h in range(n):
            sum_re, sum_im = re[0], im[0]
            for s in range(1, n):
                turn = 2.0 * math.pi * ((h * s) % n) / n
                cosine, sine = math.cos(turn), sign * math.sin(turn)
                sum_re = sum_re + re[s] * cosine - im[s] * sine
                sum_im = sum_im + im[s] * cosine + re[s] * sine
            out_re.append(sum_re)
            out_im.append(sum_im)
        return out_re, out_im
    even_re, even_im = transform(re[0::2], im[0::2], sign)
    odd_re, odd_im = transform(re[1::2], im[1::2], sign)
    half = n // 2
    out_re, out_im = [None] * n, [None] * n
    for k in range(half):
        if k == 0:
            turned_re, turned_im = odd_re[k], odd_im[k]
        elif 4 * k == n:
            turned_re, turned_im = -sign * odd_im[k], sign * odd_re[k]
        else:
            cosine = math.cos(2.0 * math.pi * k / n)
            sine = sign * math.sin(2.0 * math.pi * k / n)
            turned_re = odd_re[k] * cosine - odd_im[k] * sine
            turned_im = odd_re[k] * sine + odd_im[k] * cosine
        out_re[k], out_im[k] = even_re[k] + turned_re, even_im[k] + turned_im
        out_re[k + half] = even_re[k] - turned_re
        out_im[k + half] = even_im[k] - turned_im
    return out_re, out_im


def modal_kernel(
    nsec, ndof, steps,
    loads_ref, modes_ref, resp_ref, pattern_ref, dev_ref, eigen_ref, loss_ref, omega_ref,
    left_ref, right_ref, mine_ref, here_ref, new_ref,
    acc, held, kept_ref, after, before, send_a, recv_a, send_b, recv_b, coef, own, near,
    sl, sm, sa, ra, sb, rb, sc, rc,
):
    sec, dof = lax.axis_index("sector"), lax.axis_index("dof")
    count = nsec * ndof
    me = sec * ndof + dof
    rows, modes_all = acc.shape
    freqs, half = rows // 2, modes_all // ndof
    groups, share = half // LANES, freqs // nsec
    part = groups * share
    barrier = pltpu.get_barrier_semaphore()

    def peer(k):
        return lax.rem(me + k, count)

    def place(device):
        return {"sector": device // ndof, "dof": lax.rem(device, ndof)}

    tile = modes_ref.shape[0] // steps

    def fetch(c):
        span = pl.ds(pl.multiple_of(c * tile, tile), tile)
        return (
            pltpu.make_async_copy(loads_ref.at[:, span], held.at[:, span], sl.at[c]),
            pltpu.make_async_copy(modes_ref.at[span, :], kept_ref.at[span, :], sm.at[c]),
        )

    def begin(c, carry):
        for copy in fetch(c):
            copy.start()
        return carry

    lax.fori_loop(0, steps, begin, 0)
    acc[...] = jnp.zeros_like(acc)

    def greet(k, carry):
        pl.semaphore_signal(barrier, inc=1, device_id=place(peer(k)), device_id_type=MESH)
        return carry

    lax.fori_loop(1, count, greet, 0)

    def pick(values):
        total = None
        for d in range(ndof):
            term = jnp.where(dof == d, values[:, d * half : (d + 1) * half], 0.0)
            total = term if total is None else total + term
        return total

    def pieces():
        for kind in range(2):
            for g in range(groups):
                yield kind, g, (kind * groups + g) * share

    table = dev_ref[...]
    chosen = lax.broadcasted_iota(jnp.int32, table.shape, 0) == pattern_ref[0]
    dev_row = pick(jnp.sum(jnp.where(chosen, table, 0.0), axis=0, keepdims=True))
    scaled = dev_row * resp_ref[...]
    row = lax.rem(lax.broadcasted_iota(jnp.int32, (part, LANES), 0), share)
    omega = jnp.zeros((part, LANES), jnp.float32)
    for j in range(share):
        omega = jnp.where(row == j, omega_ref[sec * share + j], omega)

    def spread(line):
        line = pick(line)
        return jnp.concatenate(
            [
                jnp.broadcast_to(line[:, g * LANES : (g + 1) * LANES], (share, LANES))
                for g in range(groups)
            ],
            0,
        )

    loss = spread(loss_ref[...])
    for h in range(nsec):
        stiff = spread(eigen_ref[h : h + 1, :])
        shifted, damped = stiff - omega, loss * stiff
        denom = shifted * shifted + damped * damped
        coef[0, h] = shifted / denom
        coef[1, h] = damped / denom

    def multiply(c, carry):
        for copy in fetch(c):
            copy.wait()
        span = pl.ds(pl.multiple_of(c * tile, tile), tile)
        acc[...] += jnp.dot(held[:, span], kept_ref[span, :], preferred_element_type=jnp.float32)
        return carry

    lax.fori_loop(0, steps, multiply, 0)
    for d in range(ndof):
        cols = slice(d * half, (d + 1) * half)
        acc[:, cols] = acc[:, cols] - jnp.where(dof == d, scaled, 0.0)
    for t in range(nsec):
        for d in range(ndof):
            parts = []
            for kind, g, _ in pieces():
                first = kind * freqs + t * share
                left = d * half + g * LANES
                parts.append(acc[first : first + share, left : left + LANES])
            send_a[t * ndof + d] = jnp.concatenate(parts, 0).astype(jnp.bfloat16)
    pl.semaphore_wait(barrier, count - 1)

    def copy_a(to, origin):
        return pltpu.make_async_remote_copy(
            src_ref=send_a.at[to], dst_ref=recv_a.at[origin],
            send_sem=sa.at[to], recv_sem=ra.at[origin],
            device_id=place(to), device_id_type=MESH,
        )

    def copy_b(to, origin):
        return pltpu.make_async_remote_copy(
            src_ref=send_b.at[to // ndof], dst_ref=recv_b.at[origin],
            send_sem=sb.at[to], recv_sem=rb.at[origin],
            device_id=place(to), device_id_type=MESH,
        )

    def start_a(k, carry):
        copy_a(peer(k), me).start()
        return carry

    lax.fori_loop(1, count, start_a, 0)
    recv_a[pl.ds(me, 1)] = send_a[pl.ds(me, 1)]

    def wait_a(k, carry):
        copy_a(peer(k), peer(k)).wait_recv()
        return carry

    lax.fori_loop(1, count, wait_a, 0)
    rest_re, rest_im = [], []
    for s in range(nsec):
        block = recv_a[s * ndof].astype(jnp.float32)
        for d in range(1, ndof):
            block = block + recv_a[s * ndof + d].astype(jnp.float32)
        rest_re.append(block[:part])
        rest_im.append(block[part:])
    spec_re, spec_im = transform(rest_re, rest_im, -1.0)
    solved_re, solved_im = [], []
    for h in range(nsec):
        a, b = coef[0, h], coef[1, h]
        solved_re.append(spec_re[h] * a + spec_im[h] * b)
        solved_im.append(spec_im[h] * a - spec_re[h] * b)
    out_re, out_im = transform(solved_re, solved_im, 1.0)
    for s in range(nsec):
        block = jnp.concatenate([out_re[s], out_im[s]], 0) * (1.0 / nsec)
        send_b[s] = block.astype(jnp.bfloat16)

    def start_b(k, carry):
        copy_b(peer(k), me).start()
        return carry

    lax.fori_loop(1, count, start_b, 0)
    recv_b[pl.ds(me, 1)] = send_b[pl.ds(sec, 1)]

    def wait_b(k, carry):
        copy_b(peer(k), peer(k)).wait_recv()
        return carry

    lax.fori_loop(1, count, wait_b, 0)
    for t in range(nsec):
        for d in range(ndof):
            block = recv_b[t * ndof + d].astype(jnp.float32)
            for kind, g, at in pieces():
                first = kind * freqs + t * share
                left = d * half + g * LANES
                acc[first : first + share, left : left + LANES] = block[at : at + share]
    own[...] = acc[...].astype(jnp.bfloat16)

    def copy_c(side):
        to = lax.rem(sec + (nsec - 1, 1)[side], nsec)
        return pltpu.make_async_remote_copy(
            src_ref=own, dst_ref=near.at[side],
            send_sem=sc.at[side], recv_sem=rc.at[side],
            device_id={"sector": to, "dof": dof}, device_id_type=MESH,
        )

    for side in range(2):
        copy_c(side).start()
    mine_ref[...] = pick(acc[...])
    contract = (((1,), (1,)), ((), ()))

    def project(c, carry):
        span = pl.ds(pl.multiple_of(c * tile, tile), tile)
        here_ref[span, :] = lax.dot_general(
            kept_ref[span, :], own[...], contract, preferred_element_type=jnp.float32
        )
        return carry

    lax.fori_loop(0, steps, project, 0)

    def sent(k, carry):
        copy_a(peer(k), me).wait_send()
        copy_b(peer(k), me).wait_send()
        return carry

    lax.fori_loop(1, count, sent, 0)
    for side in range(2):
        copy_c(side).wait()

    def project_near(c, carry):
        span = pl.ds(pl.multiple_of(c * tile, tile), tile)
        for side, target in ((0, after), (1, before)):
            target[span, :] = lax.dot_general(
                kept_ref[span, :], near[side], contract, preferred_element_type=jnp.float32
            )
        return carry

    lax.fori_loop(0, steps, project_near, 0)
    entries = left_ref.shape[0]
    group = math.gcd(entries, 8)

    def blend(block, carry):
        for j in range(group):
            at = block * group + j
            left, right = left_ref[at], right_ref[at]
            left_new = before[pl.ds(right, 1), :] + here_ref[pl.ds(left, 1), :]
            right_new = here_ref[pl.ds(right, 1), :] + after[pl.ds(left, 1), :]
            new_ref[0, pl.ds(at, 1), :] = 0.5 * left_new
            new_ref[1, pl.ds(at, 1), :] = 0.5 * right_new
        return carry

    lax.fori_loop(0, entries // group, blend, 0)


def modal_solve(
    loads, modes, response, pattern, deviation, eigen, loss, omega_sq, left, right
):
    rows, depth = loads.shape
    modes_all = modes.shape[1]
    nsec, ndof = lax.axis_size("sector"), lax.axis_size("dof")
    half = modes_all // ndof
    count = nsec * ndof
    part = (half // LANES) * (rows // 2 // nsec)
    tile = math.gcd(depth, 1024)
    steps = depth // tile
    smem = pl.BlockSpec(memory_space=pltpu.SMEM)
    vmem = pl.BlockSpec(memory_space=pltpu.VMEM)
    away = pl.BlockSpec(memory_space=pltpu.HBM)
    block = (2 * part, LANES)
    return pl.pallas_call(
        functools.partial(modal_kernel, nsec, ndof, steps),
        out_shape=(
            jax.ShapeDtypeStruct((rows, half), jnp.float32),
            pltpu.VMEM((depth, rows), jnp.float32),
            pltpu.VMEM((2, left.shape[0], rows), jnp.float32),
        ),
        in_specs=[away, away, vmem, smem, vmem, vmem, vmem, smem, smem, smem],
        out_specs=(vmem,) * 3,
        scratch_shapes=[
            pltpu.VMEM((rows, modes_all), jnp.float32),
            pltpu.VMEM((rows, depth), jnp.bfloat16),
            pltpu.VMEM((depth, modes_all), jnp.bfloat16),
            pltpu.VMEM((depth, rows), jnp.float32),
            pltpu.VMEM((depth, rows), jnp.float32),
            pltpu.VMEM((count,) + block, jnp.bfloat16),
            pltpu.VMEM((count,) + block, jnp.bfloat16),
            pltpu.VMEM((nsec,) + block, jnp.bfloat16),
            pltpu.VMEM((count,) + block, jnp.bfloat16),
            pltpu.VMEM((2, nsec, part, LANES), jnp.float32),
            pltpu.VMEM((rows, modes_all), jnp.bfloat16),
            pltpu.VMEM((2, rows, modes_all), jnp.bfloat16),
            pltpu.SemaphoreType.DMA((steps,)),
            pltpu.SemaphoreType.DMA((steps,)),
            pltpu.SemaphoreType.DMA((count,)),
            pltpu.SemaphoreType.DMA((count,)),
            pltpu.SemaphoreType.DMA((count,)),
            pltpu.SemaphoreType.DMA((count,)),
            pltpu.SemaphoreType.DMA((2,)),
            pltpu.SemaphoreType.DMA((2,)),
        ],
        compiler_params=pltpu.CompilerParams(
            collective_id=0, has_side_effects=True, vmem_limit_bytes=LIMIT
        ),
        name="modal_solve",
    )(
        loads, modes, response, pattern, deviation, eigen, loss.reshape(1, modes_all), omega_sq,
        left, right,
    )


def recover_kernel(wide, here_in, new_ref, left_ref, right_ref, out_ref, here, buffer, sems):
    rows, depth = out_ref.shape
    contract = (((1,), (1,)), ((), ()))
    entries = left_ref.shape[0]
    group = math.gcd(entries, 8)

    def place(block, carry):
        for j in range(group):
            at = block * group + j
            here[pl.ds(left_ref[at], 1), :] = new_ref[0, pl.ds(at, 1), :]
            here[pl.ds(right_ref[at], 1), :] = new_ref[1, pl.ds(at, 1), :]
        return carry

    lax.fori_loop(0, entries // group, place, 0)
    shape = (rows, rows)
    same = lax.broadcasted_iota(jnp.int32, shape, 0) == lax.broadcasted_iota(jnp.int32, shape, 1)
    eye = jnp.where(same, 1.0, 0.0).astype(jnp.bfloat16)
    pieces = depth // wide

    def store(c):
        return pltpu.make_async_copy(
            buffer.at[c], out_ref.at[:, pl.ds(c * wide, wide)], sems.at[c]
        )

    for c in range(pieces):
        buffer[c] = lax.dot_general(
            eye,
            here[c * wide : (c + 1) * wide, :].astype(jnp.bfloat16),
            contract,
            preferred_element_type=jnp.float32,
        ).astype(jnp.bfloat16)
        store(c).start()
    for c in range(pieces):
        store(c).wait()


def recover(here, new, left, right):
    depth, rows = here.shape
    wide = math.gcd(depth, 2048)
    smem = pl.BlockSpec(memory_space=pltpu.SMEM)
    vmem = pl.BlockSpec(memory_space=pltpu.VMEM)
    return pl.pallas_call(
        functools.partial(recover_kernel, wide),
        out_shape=(
            jax.ShapeDtypeStruct((rows, depth), jnp.bfloat16),
            pltpu.VMEM((depth, rows), jnp.float32),
        ),
        in_specs=[vmem, vmem, smem, smem],
        out_specs=(pl.BlockSpec(memory_space=pl.ANY), vmem),
        input_output_aliases={0: 1},
        scratch_shapes=[
            pltpu.VMEM((depth // wide, rows, wide), jnp.bfloat16),
            pltpu.SemaphoreType.DMA((depth // wide,)),
        ],
        compiler_params=pltpu.CompilerParams(vmem_limit_bytes=LIMIT),
        name="recover",
    )(here, new, left, right)[0]


def shards(
    loads, modes, response, pattern, deviation, eigen, loss, omega_sq, iface_left, iface_right
):
    mine, here, new = modal_solve(
        loads[0], modes, response[0], pattern, deviation, eigen, loss, omega_sq,
        iface_left, iface_right,
    )
    return mine[None], recover(here, new, iface_left, iface_right)[None]


def solution(mesh):
    placed = (
        P("sector", None, "dof"),
        P("dof", None),
        P("sector", None, "dof"),
        P("sector"),
        P(),
        P(),
        P(),
        P(),
        P("dof"),
        P("dof"),
    )
    return jax.shard_map(
        shards,
        mesh=mesh,
        in_specs=placed,
        out_specs=(P("sector", None, "dof"), P("sector", None, "dof")),
        check_vma=False,
    )
```

time: 82.3 us -> 52.8 us (0.64)
  Pallas kernels: 26.3 us -> 49.9 us
  local copies, waits for them, and re-layouts: 21 us -> 1.44 us
  other arithmetic: 15.4 us -> 0 us
  matrix products: 10.4 us -> 0 us
  starting transfers between devices: 5.25 us -> 0 us
  waiting for transfers between devices: 1.96 us -> 0 us
    pallas_call x1 -> x2, Pallas kernels: 26.3 us -> 49.9 us  [the longest x1 45.5 us: modal_solve(): pl.pallas_call(functools.partial(modal_kernel, nsec, ndof, steps), out_sh...]
    scatter x2 -> x0, other arithmetic: 13.7 us -> none  [shards(): raw.at[:, :, iface_right].set(right_new).at[:, :, iface_left].set(left_new)]
    dot_general x1 -> x0, matrix products: 10.4 us -> none  [shards(): jnp.einsum('skm,dm->skd', full[None], modes, preferred_element_type=jnp.f...]
    gather x2 -> x0, local copies, waits for them, and re-layouts: 7.56 us -> none  [the longest x1 3.78 us: shards(): right_vals = jnp.take(raw, iface_right, axis=2)]
    convert_element_type x1 -> x0, local copies, waits for them, and re-layouts: 6.39 us -> none  [shards(): raw = jnp.einsum('skm,dm->skd', full[None], modes, preferred_element_type...]
    unnamed x6 -> x5, local copies, waits for them, and re-layouts: 7.06 us -> 1.44 us
    ppermute x2 -> x0, starting transfers between devices: 5.25 us -> none  [shifted_2(): lax.ppermute(shard, axis, [(i, (i + by) % size) for i in range(size)])]
    ppermute x2 -> x0, waiting for transfers between devices: 1.96 us -> none  [shifted_2(): lax.ppermute(shard, axis, [(i, (i + by) % size) for i in range(size)])]
  transfers between devices with their start and end apart: 2 -> 0, of which waited for: 1 -> 0; matrix products, arithmetic and copies ran while one was open for 13% -> 0% of each run, Pallas kernels for 0% -> 0%
where the time goes in v3:
time: 52.8 us; the launch traced here: 52.6 us
  Pallas kernels  49.9 us (95%)
  local copies, waits for them, and re-layouts  1.44 us (3%)
  between operations  1.31 us (2%)
    pallas_call x1, Pallas kernels, modal_solve(): pl.pallas_call(functools.partial(modal_kernel, nsec, ndof, steps), out_sh...  45.5 us
    pallas_call x1, Pallas kernels, recover(): pl.pallas_call(functools.partial(recover_kernel, wide), out_shape=(jax.Sh...  4.41 us
    unnamed x5, local copies, waits for them, and re-layouts  1.44 us

profile of v3, /device:TPU:0, one launch (start us, length us, event | category | flops | bytes accessed | tf_op | source)
XLA Modules:
  0.0 52.6 jit_solution(18438462530907377306)
XLA Ops:
  1.3 45.5 %modal_solve.1 = (f32[128,256]{1,0:T(8,128)}, f32[16384,128]{1,0:T(8,128)S(1)}, f32[2,512,128]{2,1,0:T(8,128)S(1)}) custom-call(bf16[128,16384]{1,0:T(8,128)(2,1)} %bitcast.5, bf16[16384,512]{1,0:T(8,128)(2,1)} %modes_ref.1, f32[128,256]{1,0:T(8,128)} %bitcast.6, s32[1]{0:T(128)S(6)} %copy.15.pattern_ref, f32[8,512]{1,0:T(8,128)} %dev_ref.1, ...), custom_call_target="tpu_custom_call" | custom-call | tf_op jit(solution)/shard_map/modal_solve/pallas_call | solution.py:293
  46.8 0.0 copy-start
  46.8 0.8 %copy-done = f32[2,512,128]{2,1,0:T(8,128)} copy-done((f32[2,512,128]{2,1,0:T(8,128)}, f32[2,512,128]{2,1,0:T(8,128)S(1)}, u32[]{:S(2)}) %copy-start) | copy-done | bytes 524312
  47.5 0.0 copy-start.1
  47.5 4.4 %recover.1 = (bf16[128,16384]{1,0:T(8,128)(2,1)}, f32[16384,128]{1,0:T(8,128)S(1)}) custom-call(f32[16384,128]{1,0:T(8,128)S(1)} %get-tuple-element.7.here_in, f32[2,512,128]{2,1,0:T(8,128)} %copy-done, s32[512]{0:T(512)} %left_ref.3, s32[512]{0:T(512)} %right_ref.3), custom_call_target="tpu_custom_call", output_to_operand_aliasing={{1}: (0, {})} | custom-call | tf_op jit(solution)/shard_map/recover/pallas_call | solution.py:375
  52.0 0.0 copy-done.1
  52.0 0.7 %copy.16 = f32[1,128,256]{2,1,0:T(8,128)} copy(f32[1,128,256]{2,1,0:T(8,128)S(1)} %bitcast.7) | data formatting | bytes 262144
Async XLA Ops:
  46.8 0.8 %copy-start = (f32[2,512,128]{2,1,0:T(8,128)}, f32[2,512,128]{2,1,0:T(8,128)S(1)}, u32[]{:S(2)}) copy-start(f32[2,512,128]{2,1,0:T(8,128)S(1)} %get-tuple-element.8.new_ref) | copy-start | bytes 1572868
  47.5 4.4 %copy-start.1 = (f32[128,256]{1,0:T(8,128)S(1)}, f32[128,256]{1,0:T(8,128)}, u32[]{:S(2)}) copy-start(f32[128,256]{1,0:T(8,128)} %get-tuple-element.6) | copy-start | bytes 393220

commit v4 on v3

--- a/solution.py
+++ b/solution.py
@@ -252,10 +252,14 @@
 
     def project_near(c, carry):
         span = pl.ds(pl.multiple_of(c * tile, tile), tile)
-        for side, target in ((0, after), (1, before)):
-            target[span, :] = lax.dot_general(
-                kept_ref[span, :], near[side], contract, preferred_element_type=jnp.float32
-            )
+        found = lax.dot_general(
+            kept_ref[span, :],
+            near[...].reshape(2 * rows, modes_all),
+            contract,
+            preferred_element_type=jnp.float32,
+        )
+        after[span, :] = found[:, :rows]
+        before[span, :] = found[:, rows:]
         return carry
 
     lax.fori_loop(0, steps, project_near, 0)

time: 52.8 us -> 49.1 us (0.930)
  Pallas kernels: 49.9 us -> 46.2 us
    pallas_call x1, Pallas kernels: 45.5 us -> 41.7 us  [modal_solve(): pl.pallas_call(functools.partial(modal_kernel, nsec, ndof, steps), out_sh...]
where the time goes in v4:
time: 49.1 us; the launch traced here: 48.9 us
  Pallas kernels  46.2 us (94%)
  local copies, waits for them, and re-layouts  1.44 us (3%)
  between operations  1.31 us (3%)
    pallas_call x1, Pallas kernels, modal_solve(): pl.pallas_call(functools.partial(modal_kernel, nsec, ndof, steps), out_sh...  41.7 us
    pallas_call x1, Pallas kernels, recover(): pl.pallas_call(functools.partial(recover_kernel, wide), out_shape=(jax.Sh...  4.41 us
    unnamed x5, local copies, waits for them, and re-layouts  1.44 us

profile of v4, /device:TPU:0, one launch (start us, length us, event | category | flops | bytes accessed | tf_op | source)
XLA Modules:
  0.0 48.9 jit_solution(8272165457195304377)
XLA Ops:
  1.3 41.7 %modal_solve.1 = (f32[128,256]{1,0:T(8,128)}, f32[16384,128]{1,0:T(8,128)S(1)}, f32[2,512,128]{2,1,0:T(8,128)S(1)}) custom-call(bf16[128,16384]{1,0:T(8,128)(2,1)} %bitcast.5, bf16[16384,512]{1,0:T(8,128)(2,1)} %modes_ref.1, f32[128,256]{1,0:T(8,128)} %bitcast.6, s32[1]{0:T(128)S(6)} %copy.15.pattern_ref, f32[8,512]{1,0:T(8,128)} %dev_ref.1, ...), custom_call_target="tpu_custom_call" | custom-call | tf_op jit(solution)/shard_map/modal_solve/pallas_call | solution.py:297
  43.0 0.0 copy-start
  43.0 0.8 %copy-done = f32[2,512,128]{2,1,0:T(8,128)} copy-done((f32[2,512,128]{2,1,0:T(8,128)}, f32[2,512,128]{2,1,0:T(8,128)S(1)}, u32[]{:S(2)}) %copy-start) | copy-done | bytes 524312
  43.8 0.0 copy-start.1
  43.8 4.4 %recover.1 = (bf16[128,16384]{1,0:T(8,128)(2,1)}, f32[16384,128]{1,0:T(8,128)S(1)}) custom-call(f32[16384,128]{1,0:T(8,128)S(1)} %get-tuple-element.7.here_in, f32[2,512,128]{2,1,0:T(8,128)} %copy-done, s32[512]{0:T(512)} %left_ref.3, s32[512]{0:T(512)} %right_ref.3), custom_call_target="tpu_custom_call", output_to_operand_aliasing={{1}: (0, {})} | custom-call | tf_op jit(solution)/shard_map/recover/pallas_call | solution.py:379
  48.2 0.0 copy-done.1
  48.2 0.7 %copy.16 = f32[1,128,256]{2,1,0:T(8,128)} copy(f32[1,128,256]{2,1,0:T(8,128)S(1)} %bitcast.7) | data formatting | bytes 262144
Async XLA Ops:
  43.0 0.8 %copy-start = (f32[2,512,128]{2,1,0:T(8,128)}, f32[2,512,128]{2,1,0:T(8,128)S(1)}, u32[]{:S(2)}) copy-start(f32[2,512,128]{2,1,0:T(8,128)S(1)} %get-tuple-element.8.new_ref) | copy-start | bytes 1572868
  43.8 4.4 %copy-start.1 = (f32[128,256]{1,0:T(8,128)S(1)}, f32[128,256]{1,0:T(8,128)}, u32[]{:S(2)}) copy-start(f32[128,256]{1,0:T(8,128)} %get-tuple-element.6) | copy-start | bytes 393220
